TPU v7x, 128 devices: a whole 4x4x4 slice. The times are simulated.
128 devices in a mesh: row: 16 (over z_hi, y, core), col: 8 (over z_lo, x).
Axes of the slice: x: 4, y: 4, z: 4 (z_hi: 2, z_lo: 2; z = z_hi * 2 + z_lo), core: 2. Of those that a mesh axis runs over, the one named last changes fastest.
Arguments:
- grad_out: bfloat16 [262144, 256], P(('row', 'col')), may hold values from -6 to 6
- preact: bfloat16 [262144, 256], P(('row', 'col')), may hold values from -6 to 6
- features: bfloat16 [262144, 256], P(('col', 'row')), may hold values from -6 to 6
- weight: bfloat16 [256, 256], replicated, may hold values from -0.375 to 0.375
- tiles: bfloat16 [16, 8, 320, 128, 128], P('row', 'col'), may hold values from -0.099609375 to 0.099609375
- tile_rows: int32 [16, 8, 320], P('row', 'col'), may hold values from 0 to 127
- tile_cols: int32 [16, 8, 320], P('row', 'col'), may hold values from 0 to 255
- live_counts: int32 [16, 8], P('row', 'col'), may hold values from 80 to 320, as said below
Outputs:
- grad_features: bfloat16 [262144, 256], P(('col', 'row'))
- grad_weight: float32 [256, 256], replicated
Inputs may be any that keep to these rules, and one draw needn't show every extreme that they name: `live_counts`: some block holds exactly 320 live tiles in every draw.
All inputs are finite; a program needn't handle non-finite values.
Results may differ from a plain program's by a relative error of at most 0.02.
Values may be sent and summed in bfloat16 or wider, within the bound.
A program may use at most 192 MiB of HBM per device.

v0:
```python
import math

import jax
import jax.numpy as jnp
from jax import lax
from jax.sharding import PartitionSpec as P


def body(grad_out, preact, features, weight, tiles, tile_rows, tile_cols, live_counts):
    width = grad_out.shape[1]
    masked = jnp.where(preact > 0, grad_out, jnp.zeros_like(grad_out))
    block = lax.all_gather(masked, "col", axis=0, tiled=True)
    row_count = block.shape[0] // 128
    row_flat = block.reshape(row_count, 128 * width)
    slots = tiles.shape[2]
    tile_stack = tiles.reshape(slots, 128, 128)
    row_index = tile_rows.reshape(slots)
    col_index = tile_cols.reshape(slots)
    count = live_counts.reshape(())
    col_tiles = lax.axis_size("row") * grad_out.shape[0] // 128
    group = math.gcd(slots, 32)
    offsets = jnp.arange(group, dtype=jnp.int32)
    row_ids = jnp.arange(row_count, dtype=jnp.int32)
    col_ids = jnp.arange(col_tiles, dtype=jnp.int32)

    def add_group(step, accum):
        start = step * group
        tile_blk = lax.dynamic_slice_in_dim(tile_stack, start, group, 0)
        rows_now = lax.dynamic_slice_in_dim(row_index, start, group, 0)
        cols_now = lax.dynamic_slice_in_dim(col_index, start, group, 0) - 0
        pick = (rows_now[:, None] == row_ids[None, :]).astype(jnp.bfloat16)
        gathered = jnp.dot(pick, row_flat, preferred_element_type=jnp.float32).astype(jnp.bfloat16)
        gathered = gathered.reshape(group, 128, width)
        prod = jnp.einsum("kab,kaf->kbf", tile_blk, gathered, preferred_element_type=jnp.float32)
        upper = prod.astype(jnp.bfloat16)
        lower = (prod - upper.astype(jnp.float32)).astype(jnp.bfloat16)
        keep = start + offsets < count
        place = ((cols_now[None, :] == col_ids[:, None]) & keep[None, :]).astype(jnp.bfloat16)
        both_place = jnp.concatenate([place, place], axis=1)
        both_vals = jnp.concatenate([upper, lower], axis=0).reshape(2 * group, 128 * width)
        return accum + jnp.dot(both_place, both_vals, preferred_element_type=jnp.float32)

    accum = jnp.zeros((col_tiles, 128 * width), jnp.float32)
    accum = lax.fori_loop(0, slots // group, add_group, accum)
    partial_value = accum.reshape(col_tiles * 128, width)
    summed = lax.psum_scatter(
        partial_value.astype(jnp.bfloat16), "row", scatter_dimension=0, tiled=True
    )
    grad_features = lax.dot_general(
        summed, weight, (((1,), (1,)), ((), ())), preferred_element_type=jnp.float32
    ).astype(jnp.bfloat16)
    weight_term = lax.dot_general(
        features, summed, (((0,), (0,)), ((), ())), preferred_element_type=jnp.float32
    )
    grad_weight = lax.psum(weight_term, ("row", "col"))
    return (grad_features, grad_weight)


def solution(mesh):
    in_specs = (
        P(("row", "col"), None),
        P(("row", "col"), None),
        P(("col", "row"), None),
        P(),
        P("row", "col", None, None, None),
        P("row", "col", None),
        P("row", "col", None),
        P("row", "col"),
    )
    out_specs = (P(("col", "row"), None), P())
    return jax.shard_map(body, mesh=mesh, in_specs=in_specs, out_specs=out_specs, check_vma=False)
```

profile of v0, /device:TPU:1, one launch (start us, length us, event | category | flops | bytes accessed | tf_op | source)
XLA Modules:
  0.0 803.8 jit_solution(6973166508205975980)
XLA Ops:
  7.2 2.7 compare_select_fusion
  10.1 14.5 %copy.12 = bf16[1,1,320,128,128]{3,4,2,1,0:T(8,128)(2,1)} copy(bf16[1,1,320,128,128]{4,3,2,1,0:T(8,128)(2,1)} %param.14) | data formatting | bytes 20971520 | tf_op args[4]
  24.6 80.9 %all-gather.2.cloned.1.call-done = bf16[16384,256]{1,0:T(8,128)(2,1)} async-done(((bf16[2048,256]{1,0:T(8,128)(2,1)}), bf16[16384,256]{1,0:T(8,128)(2,1)}) %all-gather.2.cloned.1.call-update) | async-done | bytes 8388624 | tf_op jit(solution)/shard_map/all_gather | solution.py:12
  105.4 13.4 %reshape.49 = bf16[128,32768]{1,0:T(8,128)(2,1)} reshape(bf16[16384,256]{1,0:T(8,128)(2,1)} %all-gather.2.cloned.1.call-done) | data formatting | bytes 16777216 | tf_op jit(solution)/shard_map/reshape | solution.py:14
  118.9 342.9 %while.14 = (s32[]{:T(128)}, f32[256,32768]{1,0:T(8,128)}, s32[320]{0:T(512)S(1)}, s32[]{:T(128)}, bf16[320,128,128]{1,2,0:T(8,128)(2,1)}, /*index=5*/s32[320]{0...) while((s32[]{:T(128)}, f32[256,32768]{1,0:T(8,128)}, ...), condition=%wide.region_1.2_spmd.clone, body=%wide.region_0.1_spmd.clone.sunk | while | flops 1634766848 | bytes 110117888 | solution.py:44
  119.8 4.6 convolution_convert_fusion.3
  124.9 1.9 subtract_convert_fusion.2
  127.3 2.6 copy.19
  129.8 12.4 %convolution_add_fusion.2 = f32[256,32768]{1,0:T(8,128)} fusion(bf16[64,32768]{1,0:T(8,128)(2,1)S(1)} %bitcast.29, f32[256,32768]{1,0:T(8,128)} %get-tuple-element.281, pred[]{:T(512)S(6)} %compare.3, pred[256,32]{0,1:T(32,128)(4,1)S(1)} %fusion.34), kind=kOutput, calls=%fused_computation.3.clone.1 | convolution fusion | flops 1090535424 | bytes 71311360 | tf_op jit(solution)/shard_map/while/body/eval_jaxpr/dot_general | solution.py:41
  143.2 4.6 convolution_convert_fusion.3
  148.3 1.9 subtract_convert_fusion.2
  150.6 2.6 copy.19
  153.2 24.6 %convolution_add_fusion.2 = f32[256,32768]{1,0:T(8,128)} fusion(bf16[64,32768]{1,0:T(8,128)(2,1)S(1)} %bitcast.29, f32[256,32768]{1,0:T(8,128)} %get-tuple-element.281, pred[]{:T(512)S(6)} %compare.3, pred[256,32]{0,1:T(32,128)(4,1)S(1)} %fusion.34), kind=kOutput, calls=%fused_computation.3.clone.1 | convolution fusion | flops 1090535424 | bytes 71311360 | tf_op jit(solution)/shard_map/while/body/eval_jaxpr/dot_general | solution.py:41
  178.7 4.6 convolution_convert_fusion.3
  183.8 1.9 subtract_convert_fusion.2
  186.1 2.6 copy.19
  188.7 24.6 %convolution_add_fusion.2 = f32[256,32768]{1,0:T(8,128)} fusion(bf16[64,32768]{1,0:T(8,128)(2,1)S(1)} %bitcast.29, f32[256,32768]{1,0:T(8,128)} %get-tuple-element.281, pred[]{:T(512)S(6)} %compare.3, pred[256,32]{0,1:T(32,128)(4,1)S(1)} %fusion.34), kind=kOutput, calls=%fused_computation.3.clone.1 | convolution fusion | flops 1090535424 | bytes 71311360 | tf_op jit(solution)/shard_map/while/body/eval_jaxpr/dot_general | solution.py:41
  214.2 4.6 convolution_convert_fusion.3
  219.3 1.9 subtract_convert_fusion.2
  221.6 2.6 copy.19
  224.2 24.6 %convolution_add_fusion.2 = f32[256,32768]{1,0:T(8,128)} fusion(bf16[64,32768]{1,0:T(8,128)(2,1)S(1)} %bitcast.29, f32[256,32768]{1,0:T(8,128)} %get-tuple-element.281, pred[]{:T(512)S(6)} %compare.3, pred[256,32]{0,1:T(32,128)(4,1)S(1)} %fusion.34), kind=kOutput, calls=%fused_computation.3.clone.1 | convolution fusion | flops 1090535424 | bytes 71311360 | tf_op jit(solution)/shard_map/while/body/eval_jaxpr/dot_general | solution.py:41
  249.7 4.6 convolution_convert_fusion.3
  254.8 1.9 subtract_convert_fusion.2
  257.1 2.6 copy.19
  259.7 24.6 %convolution_add_fusion.2 = f32[256,32768]{1,0:T(8,128)} fusion(bf16[64,32768]{1,0:T(8,128)(2,1)S(1)} %bitcast.29, f32[256,32768]{1,0:T(8,128)} %get-tuple-element.281, pred[]{:T(512)S(6)} %compare.3, pred[256,32]{0,1:T(32,128)(4,1)S(1)} %fusion.34), kind=kOutput, calls=%fused_computation.3.clone.1 | convolution fusion | flops 1090535424 | bytes 71311360 | tf_op jit(solution)/shard_map/while/body/eval_jaxpr/dot_general | solution.py:41
  285.2 4.6 convolution_convert_fusion.3
  290.3 1.9 subtract_convert_fusion.2
  292.6 2.6 copy.19
  295.2 24.6 %convolution_add_fusion.2 = f32[256,32768]{1,0:T(8,128)} fusion(bf16[64,32768]{1,0:T(8,128)(2,1)S(1)} %bitcast.29, f32[256,32768]{1,0:T(8,128)} %get-tuple-element.281, pred[]{:T(512)S(6)} %compare.3, pred[256,32]{0,1:T(32,128)(4,1)S(1)} %fusion.34), kind=kOutput, calls=%fused_computation.3.clone.1 | convolution fusion | flops 1090535424 | bytes 71311360 | tf_op jit(solution)/shard_map/while/body/eval_jaxpr/dot_general | solution.py:41
  320.7 4.6 convolution_convert_fusion.3
  325.8 1.9 subtract_convert_fusion.2
  328.1 2.6 copy.19
  330.7 24.6 %convolution_add_fusion.2 = f32[256,32768]{1,0:T(8,128)} fusion(bf16[64,32768]{1,0:T(8,128)(2,1)S(1)} %bitcast.29, f32[256,32768]{1,0:T(8,128)} %get-tuple-element.281, pred[]{:T(512)S(6)} %compare.3, pred[256,32]{0,1:T(32,128)(4,1)S(1)} %fusion.34), kind=kOutput, calls=%fused_computation.3.clone.1 | convolution fusion | flops 1090535424 | bytes 71311360 | tf_op jit(solution)/shard_map/while/body/eval_jaxpr/dot_general | solution.py:41
  356.2 4.6 convolution_convert_fusion.3
  363.6 2.6 copy.19
  366.2 24.6 %convolution_add_fusion.2 = f32[256,32768]{1,0:T(8,128)} fusion(bf16[64,32768]{1,0:T(8,128)(2,1)S(1)} %bitcast.29, f32[256,32768]{1,0:T(8,128)} %get-tuple-element.281, pred[]{:T(512)S(6)} %compare.3, pred[256,32]{0,1:T(32,128)(4,1)S(1)} %fusion.34), kind=kOutput, calls=%fused_computation.3.clone.1 | convolution fusion | flops 1090535424 | bytes 71311360 | tf_op jit(solution)/shard_map/while/body/eval_jaxpr/dot_general | solution.py:41
  391.7 4.6 convolution_convert_fusion.3
  399.2 2.6 copy.19
  401.7 24.6 %convolution_add_fusion.2 = f32[256,32768]{1,0:T(8,128)} fusion(bf16[64,32768]{1,0:T(8,128)(2,1)S(1)} %bitcast.29, f32[256,32768]{1,0:T(8,128)} %get-tuple-element.281, pred[]{:T(512)S(6)} %compare.3, pred[256,32]{0,1:T(32,128)(4,1)S(1)} %fusion.34), kind=kOutput, calls=%fused_computation.3.clone.1 | convolution fusion | flops 1090535424 | bytes 71311360 | tf_op jit(solution)/shard_map/while/body/eval_jaxpr/dot_general | solution.py:41
  427.2 4.6 convolution_convert_fusion.3
  434.7 2.6 copy.19
  437.2 24.6 %convolution_add_fusion.2 = f32[256,32768]{1,0:T(8,128)} fusion(bf16[64,32768]{1,0:T(8,128)(2,1)S(1)} %bitcast.29, f32[256,32768]{1,0:T(8,128)} %get-tuple-element.281, pred[]{:T(512)S(6)} %compare.3, pred[256,32]{0,1:T(32,128)(4,1)S(1)} %fusion.34), kind=kOutput, calls=%fused_computation.3.clone.1 | convolution fusion | flops 1090535424 | bytes 71311360 | tf_op jit(solution)/shard_map/while/body/eval_jaxpr/dot_general | solution.py:41
  461.8 17.1 %convert_element_type.45 = bf16[256,32768]{1,0:T(8,128)(2,1)} convert(f32[256,32768]{1,0:T(8,128)} %get-tuple-element.171) | non-fusion elementwise | flops 8388608 | bytes 50331648 | tf_op jit(solution)/shard_map/convert_element_type | solution.py:47
  478.9 25.6 %convert_element_type.46 = bf16[32768,256]{1,0:T(8,128)(2,1)} reshape(bf16[256,32768]{1,0:T(8,128)(2,1)} %convert_element_type.45) | data formatting | bytes 33554432 | tf_op jit(solution)/shard_map/convert_element_type | solution.py:47
  504.6 145.1 %reduce-scatter.2.cloned.1.call-done = bf16[2048,256]{1,0:T(8,128)(2,1)} async-done(((bf16[32768,256]{1,0:T(8,128)(2,1)}), bf16[2048,256]{1,0:T(8,128)(2,1)}) %reduce-scatter.2.cloned.1.call-update) | async-done | bytes 1048592 | tf_op jit(solution)/shard_map/reduce_scatter | solution.py:46
  649.7 2.4 convolution_bitcast_fusion
  652.1 2.7 convolution_convert_fusion.1
  654.8 140.8 %all-reduce.2.cloned.1.call-done = f32[256,256]{0,1:T(8,128)} async-done(((f32[256,256]{0,1:T(8,128)}), f32[256,256]{0,1:T(8,128)}) %all-reduce.2.cloned.1.call-update) | async-done | bytes 262160 | tf_op jit(solution)/shard_map/psum | solution.py:55
  (81 shorter events, 25.2 us)
Async XLA Ops:
  7.2 642.5 %copy-start = (bf16[2048,256]{1,0:T(8,128)(2,1)S(1)}, bf16[2048,256]{1,0:T(8,128)(2,1)}, u32[]{:S(2)}) copy-start(bf16[2048,256]{1,0:T(8,128)(2,1)} %param.12) | copy-start | bytes 3145732
  7.2 2.9 copy-start.2
  7.2 2.9 copy-start.3
  7.2 98.2 %all-gather.2.cloned.1.call-start = ((), (), s32[]{:S(2)}) async-start(), calls=%async_computation.1 | async-start | bytes 9437184 | tf_op jit(solution)/shard_map/all_gather | solution.py:12
  10.0 639.7 %reduce-scatter.2.cloned.1.call-start = ((), (), s32[]{:S(2)}) async-start(), calls=%async_computation.2 | async-start | bytes 17825792 | tf_op jit(solution)/shard_map/reduce_scatter | solution.py:46
  504.5 147.6 %copy-start.1 = (bf16[256,256]{1,0:T(8,128)(2,1)S(1)}, bf16[256,256]{1,0:T(8,128)(2,1)}, u32[]{:S(2)}) copy-start(bf16[256,256]{1,0:T(8,128)(2,1)} %param.13) | copy-start | bytes 393220
  504.6 291.0 %all-reduce.2.cloned.1.call-start = ((), (), s32[]{:S(2)}) async-start(), calls=%async_computation.3 | async-start | bytes 524288 | tf_op jit(solution)/shard_map/psum | solution.py:55
Sparse Core Ops, SparseCore 0:
  10.3 95.1 all-gather.1
  504.7 144.9 reduce-scatter.1
  655.7 139.7 all-reduce.1
where the time goes:
time: 806 us; the launch traced here: 804 us
  waiting for transfers between devices  367 us (46%)
  matrix products  304 us (38%)
  local copies, waits for them, and re-layouts  87.5 us (11%)
  other arithmetic  30.8 us (4%)
  between operations  13.8 us (2%)
    dot_general x10, matrix products, add_group(): jnp.dot(both_place, both_vals, preferred_element_type=jnp.float32)  234 us
    reduce_scatter x1, waiting for transfers between devices, body(): lax.psum_scatter(partial_value.astype(jnp.bfloat16), 'row', scatter_dimen...  145 us
    psum x1, waiting for transfers between devices, body(): grad_weight = lax.psum(weight_term, ('row', 'col'))  141 us
    all_gather x1, waiting for transfers between devices, body(): block = lax.all_gather(masked, 'col', axis=0, tiled=True)  80.9 us
    dot_general x10, matrix products, add_group(): jnp.dot(pick, row_flat, preferred_element_type=jnp.float32)  46.4 us
    while x20, local copies, waits for them, and re-layouts  30.6 us
    convert_element_type x1, local copies, waits for them, and re-layouts, body(): partial_value.astype(jnp.bfloat16)  25.6 us
    dot_general x10, matrix products, add_group(): jnp.einsum('kab,kaf->kbf', tile_blk, gathered, preferred_element_type=jnp...  19.4 us
  transfers between devices with their start and end apart: 3, of which 3 were waited for; matrix products, arithmetic and copies ran while one was open for 2% of the time, Pallas kernels for 0%

commit v1 on v0

v1 whole, which is shorter than its diff:
```python
import functools

import jax
import jax.numpy as jnp
from jax import lax
from jax.experimental import pallas as pl
from jax.experimental.pallas import tpu as pltpu
from jax.sharding import PartitionSpec as P

MESH = pl.DeviceIdType.MESH
GROUP = 8
STAGE = 16


def block_kernel(rows_ref, cols_ref, count_ref, block_hbm, tiles_hbm, out_hbm,
                 block, acc, tile_buf, stage, block_sem, tile_sem, out_sem):
    slots = tiles_hbm.shape[0]
    groups = slots // GROUP
    depth = tile_buf.shape[0]
    parts = block_sem.shape[0]
    part = block.shape[0] // parts
    count = count_ref[0]
    live_groups = lax.div(count + (GROUP - 1), GROUP)

    def tile_copy(g, slot):
        return pltpu.make_async_copy(
            tiles_hbm.at[pl.ds(g * GROUP, GROUP)], tile_buf.at[slot], tile_sem.at[slot])

    def block_copy(p):
        return pltpu.make_async_copy(
            block_hbm.at[pl.ds(p * part, part)], block.at[pl.ds(p * part, part)], block_sem.at[p])

    for p in range(parts):
        block_copy(p).start()
    for s in range(depth - 1):
        @pl.when(s < live_groups)
        def _():
            tile_copy(s, s).start()

    zero = jnp.zeros(acc.shape[1:], jnp.float32)

    def clear(i, carry):
        acc[i] = zero
        return carry

    lax.fori_loop(0, acc.shape[0], clear, 0)
    for p in range(parts):
        block_copy(p).wait()

    def step(g, carry):
        slot = lax.rem(g, depth)
        ahead = g + depth - 1

        @pl.when(ahead < live_groups)
        def _():
            tile_copy(ahead, lax.rem(ahead, depth)).start()

        tile_copy(g, slot).wait()
        prods = []
        for u in range(GROUP):
            k = g * GROUP + u
            tile = tile_buf[slot, u]
            vals = block[rows_ref[k]]
            prods.append(lax.dot_general(
                tile, vals, (((0,), (0,)), ((), ())), preferred_element_type=jnp.float32))
        for u in range(GROUP):
            k = g * GROUP + u
            c = cols_ref[k]
            keep = jnp.where(k < count, 1.0, 0.0).astype(jnp.float32)
            acc[c] = acc[c] + prods[u] * keep
        return carry

    lax.fori_loop(0, live_groups, step, 0)

    pieces = acc.shape[0] // STAGE

    def out_copy(i, slot):
        return pltpu.make_async_copy(
            stage.at[slot], out_hbm.at[pl.ds(i * STAGE, STAGE)], out_sem.at[slot])

    def emit(i, carry):
        slot = lax.rem(i, 2)

        @pl.when(i >= 2)
        def _():
            out_copy(i - 2, slot).wait()

        for u in range(STAGE):
            stage[slot, u] = acc[i * STAGE + u].astype(jnp.bfloat16)
        out_copy(i, slot).start()
        return carry

    lax.fori_loop(0, pieces, emit, 0)
    out_copy(pieces - 2, lax.rem(pieces - 2, 2)).wait()
    out_copy(pieces - 1, lax.rem(pieces - 1, 2)).wait()


def block_product(block, tiles, rows, cols, count, col_tiles):
    row_tiles, side, width = block.shape
    slots = tiles.shape[0]
    return pl.pallas_call(
        block_kernel,
        name="block_product",
        grid_spec=pltpu.PrefetchScalarGridSpec(
            num_scalar_prefetch=3,
            grid=(1,),
            in_specs=[pl.BlockSpec(memory_space=pl.ANY)] * 2,
            out_specs=pl.BlockSpec(memory_space=pl.ANY),
            scratch_shapes=[
                pltpu.VMEM((row_tiles, side, width), jnp.bfloat16),
                pltpu.VMEM((col_tiles, side, width), jnp.float32),
                pltpu.VMEM((6, GROUP, side, side), jnp.bfloat16),
                pltpu.VMEM((2, STAGE, side, width), jnp.bfloat16),
                pltpu.SemaphoreType.DMA((4,)),
                pltpu.SemaphoreType.DMA((6,)),
                pltpu.SemaphoreType.DMA((2,)),
            ],
        ),
        out_shape=jax.ShapeDtypeStruct((col_tiles, side, width), jnp.bfloat16),
        compiler_params=pltpu.CompilerParams(
            dimension_semantics=("arbitrary",), vmem_limit_bytes=56 * 1024 * 1024),
        cost_estimate=pl.CostEstimate(
            flops=2 * slots * side * side * width, transcendentals=0,
            bytes_accessed=2 * (block.size + tiles.size + col_tiles * side * width)),
    )(rows, cols, count, block, tiles)


def place():
    r, q = lax.axis_index("row"), lax.axis_index("col")
    core, y, z_hi = lax.rem(r, 2), lax.rem(lax.div(r, 2), 4), lax.div(r, 8)
    x, z_lo = lax.rem(q, 4), lax.div(q, 4)
    return core, x, y, z_hi, z_lo


def device(core, x, y, z_hi, z_lo):
    return ((z_hi * 4 + y) * 2 + core, z_lo * 4 + x)


def meet(partners):
    barrier = pltpu.get_barrier_semaphore()
    for partner in partners:
        pl.semaphore_signal(barrier, inc=1, device_id=partner, device_id_type=MESH)
    pl.semaphore_wait(barrier, len(partners))


def gather_kernel(grad_ref, preact_ref, out_hbm, masked, local_sem, send_sem, recv_sem):
    core, x, y, z_hi, z_lo = place()
    tiles = masked.shape[0]
    half = tiles // 2
    right = device(core, lax.rem(x + 1, 4), y, z_hi, z_lo)
    left = device(core, lax.rem(x + 3, 4), y, z_hi, z_lo)
    over = device(core, x, y, z_hi, 1 - z_lo)

    def rows(z_at, x_at, part):
        return pl.ds((z_at * 4 + x_at) * tiles + part * half, half)

    grads = grad_ref[...]
    masked[...] = jnp.where(preact_ref[...] > 0, grads, jnp.zeros_like(grads))
    meet([right, left, over])

    def send(n, source, z_at, x_at, part, target):
        spot = rows(z_at, x_at, part)
        copy = pltpu.make_async_remote_copy(
            src_ref=masked.at[pl.ds(part * half, half)] if source is None else out_hbm.at[spot],
            dst_ref=out_hbm.at[spot], send_sem=send_sem.at[n], recv_sem=recv_sem.at[n],
            device_id=target, device_id_type=MESH)
        copy.start()
        return copy

    x_r, x_l, x_o = lax.rem(x + 1, 4), lax.rem(x + 3, 4), lax.rem(x + 2, 4)
    other = 1 - z_lo
    copies = {}
    copies[0] = send(0, None, z_lo, x, 0, right)
    copies[1] = send(1, None, z_lo, x, 1, left)
    copies[2] = send(2, None, z_lo, x, 0, over)
    copies[3] = send(3, None, z_lo, x, 1, over)
    copies[4] = send(4, None, z_lo, x, 1, right)
    copies[5] = send(5, None, z_lo, x, 0, left)
    own = pltpu.make_async_copy(
        masked, out_hbm.at[pl.ds((z_lo * 4 + x) * tiles, tiles)], local_sem)
    own.start()
    copies[0].wait_recv()
    copies[6] = send(6, 1, z_lo, x_l, 0, right)
    copies[1].wait_recv()
    copies[7] = send(7, 1, z_lo, x_r, 1, left)
    copies[2].wait_recv()
    copies[8] = send(8, 1, other, x, 0, right)
    copies[9] = send(9, 1, other, x, 0, left)
    copies[3].wait_recv()
    copies[10] = send(10, 1, other, x, 1, right)
    copies[11] = send(11, 1, other, x, 1, left)
    copies[6].wait_recv()
    copies[12] = send(12, 1, z_lo, x_o, 0, over)
    copies[7].wait_recv()
    copies[13] = send(13, 1, z_lo, x_o, 1, over)
    for n in (4, 5, 8, 9, 10, 11, 12, 13):
        copies[n].wait_recv()
    for n in range(14):
        copies[n].wait_send()
    own.wait()


def gather_rows(grad_out, preact, members):
    tiles, side, width = grad_out.shape
    return pl.pallas_call(
        gather_kernel,
        name="gather_rows",
        in_specs=[pl.BlockSpec(memory_space=pltpu.VMEM)] * 2,
        out_specs=pl.BlockSpec(memory_space=pl.ANY),
        out_shape=jax.ShapeDtypeStruct((members * tiles, side, width), jnp.bfloat16),
        scratch_shapes=[
            pltpu.VMEM((tiles, side, width), jnp.bfloat16),
            pltpu.SemaphoreType.DMA,
            pltpu.SemaphoreType.DMA((14,)),
            pltpu.SemaphoreType.DMA((14,)),
        ],
        compiler_params=pltpu.CompilerParams(
            collective_id=1, has_side_effects=True, vmem_limit_bytes=60 * 1024 * 1024),
    )(grad_out, preact)


ORDER = tuple((s, d) for s in (0, 1) for d in (2, 1, 3, 0))


def reduce_kernel(part_hbm, features_ref, weight_ref, grad_ref, gw_ref,
                  own, core_in, far_l, far_r, near_l, near_r, relay, cross,
                  term, core_half, plane_in, z_in, halves,
                  load_sem, send_sem, recv_sem, ar_send, ar_recv):
    core, x, y, z_hi, z_lo = place()
    tiles = own.shape[1]
    half = tiles // 2
    z = z_hi * 2 + z_lo

    def at_z(zz):
        return device(core, x, y, lax.div(zz, 2), lax.rem(zz, 2))

    mate = device(1 - core, x, y, z_hi, z_lo)
    right = device(core, x, lax.rem(y + 1, 4), z_hi, z_lo)
    left = device(core, x, lax.rem(y + 3, 4), z_hi, z_lo)
    above, below = at_z(lax.rem(z + 1, 4)), at_z(lax.rem(z + 3, 4))
    plane = [device(core, lax.rem(x + d % 4, 4), lax.rem(y + d // 4, 4), z_hi, z_lo)
             for d in range(1, 16)]
    column = [at_z(lax.rem(z + d, 4)) for d in range(1, 4)]

    def chunk(s, d, c):
        z_to = 1 - z_hi if s == 0 else z_hi
        return pl.ds(((z_to * 4 + lax.rem(y + d, 4)) * 2 + c) * tiles, tiles)

    loads = [pltpu.make_async_copy(part_hbm.at[chunk(s, d, core)], own.at[s * 4 + d], load_sem.at[n])
             for n, (s, d) in enumerate(ORDER)]
    for load in loads[:4]:
        load.start()
    meet([mate] + plane + column)

    def remote(n, source, target_ref, target):
        return pltpu.make_async_remote_copy(
            src_ref=source, dst_ref=target_ref, send_sem=send_sem.at[n], recv_sem=recv_sem.at[n],
            device_id=target, device_id_type=MESH)

    swaps = [remote(n, part_hbm.at[chunk(s, d, 1 - core)], core_in.at[s * 4 + d], mate)
             for n, (s, d) in enumerate(ORDER)]
    ahead = 3
    for swap in swaps[:ahead]:
        swap.start()

    def add_into(dst, dst_at, src, src_at, count):
        def one(t, carry):
            dst[dst_at[0], dst_at[1] + t] = (
                dst[dst_at[0], dst_at[1] + t].astype(jnp.float32)
                + src[src_at[0], src_at[1] + t].astype(jnp.float32)).astype(jnp.bfloat16)
            return carry
        lax.fori_loop(0, count, one, 0)

    def settle(n):
        s, d = ORDER[n]
        if n + ahead < len(ORDER):
            swaps[n + ahead].start()
        if n + 4 < len(ORDER):
            loads[n + 4].start()
        loads[n].wait()
        swaps[n].wait_recv()
        add_into(own, (s * 4 + d, 0), core_in, (s * 4 + d, 0), tiles)

    low, high = pl.ds(0, half), pl.ds(half, half)
    sent = list(swaps)

    def go(n, source, target_ref, target):
        copy = remote(n, source, target_ref, target)
        copy.start()
        sent.append(copy)
        return copy

    far, direct, merged = {}, {}, {}

    def spread(s):
        first = s * 4
        base = 8 + s * 6
        settle(first)
        far[s] = (go(base, own.at[s * 4 + 2, low], far_l.at[s], right),
                  go(base + 1, own.at[s * 4 + 2, high], far_r.at[s], left))
        settle(first + 1)
        one = go(base + 2, own.at[s * 4 + 1, high], near_l.at[s, high], right)
        settle(first + 2)
        two = go(base + 3, own.at[s * 4 + 3, low], near_r.at[s, low], left)
        direct[s] = (one, two)
        settle(first + 3)

    def forward(s):
        base = 8 + s * 6
        far[s][0].wait_recv()
        add_into(own, (s * 4 + 1, 0), far_l, (s, 0), half)
        one = go(base + 4, own.at[s * 4 + 1, low], near_l.at[s, low], right)
        far[s][1].wait_recv()
        add_into(own, (s * 4 + 3, half), far_r, (s, 0), half)
        two = go(base + 5, own.at[s * 4 + 3, high], near_r.at[s, high], left)
        merged[s] = (one, two)

    spread(0)
    forward(0)
    spread(1)

    def three(t):
        return (own[0, t].astype(jnp.float32) + near_l[0, t].astype(jnp.float32)
                + near_r[0, t].astype(jnp.float32)).astype(jnp.bfloat16)

    def close(start):
        def one(t, carry):
            own[0, start + t] = three(start + t)
            return carry
        lax.fori_loop(0, half, one, 0)

    merged[0][0].wait_recv()
    direct[0][1].wait_recv()
    close(0)
    up = go(20, own.at[0, low], relay.at[0], above)
    merged[0][1].wait_recv()
    direct[0][0].wait_recv()
    close(half)
    down = go(21, own.at[0, high], relay.at[1], below)
    forward(1)
    up.wait_recv()
    up_end = go(22, relay.at[0], cross.at[0], above)
    down.wait_recv()
    down_end = go(23, relay.at[1], cross.at[1], below)

    term[...] = jnp.zeros_like(term)
    pair = 4

    def finish(part):
        def one(g, carry):
            t = part * half + g * pair
            spot = pl.ds(t, pair)
            total = (own[4, spot].astype(jnp.float32) + near_l[1, spot].astype(jnp.float32)
                     + near_r[1, spot].astype(jnp.float32)
                     + cross[part, pl.ds(g * pair, pair)].astype(jnp.float32))
            summed = total.astype(jnp.bfloat16).reshape(pair * total.shape[1], total.shape[2])
            grads = lax.dot_general(summed, weight_ref[...], (((1,), (1,)), ((), ())),
                                    preferred_element_type=jnp.float32)
            grad_ref[spot] = grads.astype(jnp.bfloat16).reshape(total.shape)
            feats = features_ref[spot].reshape(summed.shape)
            term[...] += lax.dot_general(feats, summed, (((0,), (0,)), ((), ())),
                                         preferred_element_type=jnp.float32)
            return carry
        lax.fori_loop(0, half // pair, one, 0)

    merged[1][0].wait_recv()
    direct[1][1].wait_recv()
    up_end.wait_recv()
    finish(0)
    merged[1][1].wait_recv()
    direct[1][0].wait_recv()
    down_end.wait_recv()
    finish(1)

    def tiny(n, source, target_ref, target):
        copy = pltpu.make_async_remote_copy(
            src_ref=source, dst_ref=target_ref, send_sem=ar_send.at[n], recv_sem=ar_recv.at[n],
            device_id=target, device_id_type=MESH)
        copy.start()
        sent.append(copy)
        return copy

    lines = core_half.shape[0]
    piece = lines // 16
    spot = y * 4 + x

    def piece_of(p):
        return pl.ds(pl.multiple_of(p * piece, piece), piece)

    def side_of(c):
        return pl.ds(pl.multiple_of(c * lines, lines), lines)

    swap = tiny(0, term.at[side_of(1 - core)], core_half, mate)
    swap.wait_recv()
    halves[...] = term[side_of(core), :] + core_half[...]
    spots = [lax.rem(y + d // 4, 4) * 4 + lax.rem(x + d % 4, 4) for d in range(1, 16)]
    out = [tiny(d, halves.at[piece_of(spots[d - 1])], plane_in.at[d - 1], plane[d - 1])
           for d in range(1, 16)]
    total = halves[piece_of(spot), :]
    for d in range(1, 16):
        out[d - 1].wait_recv()
        total = total + plane_in[d - 1]
    z_in[z] = total
    ups = [tiny(15 + d, z_in.at[z], z_in.at[z], column[d - 1]) for d in range(1, 4)]
    for copy in ups:
        copy.wait_recv()
    total = (z_in[0] + z_in[1]) + (z_in[2] + z_in[3])
    mine = pl.ds(pl.multiple_of(core * lines + spot * piece, piece), piece)
    gw_ref[mine, :] = total
    out = [tiny(18 + d, gw_ref.at[mine], gw_ref.at[mine], plane[d - 1]) for d in range(1, 16)]
    for copy in out:
        copy.wait_recv()
    swap = tiny(34, gw_ref.at[side_of(core)], gw_ref.at[side_of(core)], mate)
    swap.wait_recv()
    for copy in sent:
        copy.wait_send()


def reduce_finish(partial_value, features, weight):
    tiles, side, width = features.shape
    depth = weight.shape[0]
    block = (tiles, side, width)
    half = (tiles // 2, side, width)
    return pl.pallas_call(
        reduce_kernel,
        name="reduce_finish",
        in_specs=[pl.BlockSpec(memory_space=pl.ANY)] + [pl.BlockSpec(memory_space=pltpu.VMEM)] * 2,
        out_specs=[pl.BlockSpec(memory_space=pltpu.VMEM)] * 2,
        out_shape=[jax.ShapeDtypeStruct(block, jnp.bfloat16),
                   jax.ShapeDtypeStruct((depth, width), jnp.float32)],
        scratch_shapes=[
            pltpu.VMEM((8,) + block, jnp.bfloat16),
            pltpu.VMEM((8,) + block, jnp.bfloat16),
            pltpu.VMEM((2,) + half, jnp.bfloat16),
            pltpu.VMEM((2,) + half, jnp.bfloat16),
            pltpu.VMEM((2,) + block, jnp.bfloat16),
            pltpu.VMEM((2,) + block, jnp.bfloat16),
            pltpu.VMEM((2,) + half, jnp.bfloat16),
            pltpu.VMEM((2,) + half, jnp.bfloat16),
            pltpu.VMEM((depth, width), jnp.float32),
            pltpu.VMEM((depth // 2, width), jnp.float32),
            pltpu.VMEM((15, depth // 32, width), jnp.float32),
            pltpu.VMEM((4, depth // 32, width), jnp.float32),
            pltpu.VMEM((depth // 2, width), jnp.float32),
            pltpu.SemaphoreType.DMA((8,)),
            pltpu.SemaphoreType.DMA((24,)),
            pltpu.SemaphoreType.DMA((24,)),
            pltpu.SemaphoreType.DMA((35,)),
            pltpu.SemaphoreType.DMA((35,)),
        ],
        compiler_params=pltpu.CompilerParams(
            collective_id=0, has_side_effects=True, vmem_limit_bytes=60 * 1024 * 1024),
    )(partial_value, features, weight)


def body(grad_out, preact, features, weight, tiles, tile_rows, tile_cols, live_counts):
    nodes, width = grad_out.shape
    side = tiles.shape[-1]
    slots = tiles.shape[2]
    shape = (nodes // side, side, width)
    block = gather_rows(grad_out.reshape(shape), preact.reshape(shape), lax.axis_size("col"))
    col_tiles = lax.axis_size("row") * nodes // side
    partial_value = block_product(
        block, tiles.reshape(slots, side, side),
        tile_rows.reshape(slots), tile_cols.reshape(slots), live_counts.reshape(1), col_tiles)
    grad_features, grad_weight = reduce_finish(partial_value, features.reshape(shape), weight)
    return (grad_features.reshape(nodes, width), grad_weight)


def solution(mesh):
    in_specs = (
        P(("row", "col"), None),
        P(("row", "col"), None),
        P(("col", "row"), None),
        P(),
        P("row", "col", None, None, None),
        P("row", "col", None),
        P("row", "col", None),
        P("row", "col"),
    )
    out_specs = (P(("col", "row"), None), P())
    return jax.shard_map(body, mesh=mesh, in_specs=in_specs, out_specs=out_specs, check_vma=False)
```

time: 806 us -> 198 us (0.25)
  waiting for transfers between devices: 367 us -> 0 us
  matrix products: 304 us -> 0 us
  Pallas kernels: 0 us -> 190 us
  local copies, waits for them, and re-layouts: 87.5 us -> 3.93 us
  other arithmetic: 30.8 us -> 2.55 us
  between operations: 13.8 us -> 1.3 us
    dot_general x32 -> x0, matrix products: 304 us -> none  [the longest x10 234 us: add_group(): jnp.dot(both_place, both_vals, preferred_element_type=jnp.float32)]
    pallas_call x0 -> x3, Pallas kernels: none -> 190 us  [the longest x1 103 us: reduce_finish(): pl.pallas_call(reduce_kernel, name='reduce_finish', in_specs=[pl.BlockSpe...]
    reduce_scatter x1 -> x0, waiting for transfers between devices: 145 us -> none  [body(): lax.psum_scatter(partial_value.astype(jnp.bfloat16), 'row', scatter_dimen...]
    psum x1 -> x0, waiting for transfers between devices: 141 us -> none  [body(): grad_weight = lax.psum(weight_term, ('row', 'col'))]
    all_gather x1 -> x0, waiting for transfers between devices: 80.9 us -> none  [body(): block = lax.all_gather(masked, 'col', axis=0, tiled=True)]
    while x20 -> x0, local copies, waits for them, and re-layouts: 30.6 us -> none
    convert_element_type x1 -> x0, local copies, waits for them, and re-layouts: 25.6 us -> none  [body(): partial_value.astype(jnp.bfloat16)]
    convert_element_type x1 -> x0, other arithmetic: 17.1 us -> none  [body(): partial_value.astype(jnp.bfloat16)]
  transfers between devices with their start and end apart: 3 -> 0, of which waited for: 3 -> 0; matrix products, arithmetic and copies ran while one was open for 2% -> 0% of each run, Pallas kernels for 0% -> 0%
where the time goes in v1:
time: 198 us
  Pallas kernels  190 us (96%)
  local copies, waits for them, and re-layouts  3.93 us (2%)
  other arithmetic  2.55 us (1%)
    pallas_call x1, Pallas kernels, reduce_finish(): pl.pallas_call(reduce_kernel, name='reduce_finish', in_specs=[pl.BlockSpe...  103 us
    pallas_call x1, Pallas kernels, gather_rows(): pl.pallas_call(gather_kernel, name='gather_rows', in_specs=[pl.BlockSpec(...  63.3 us
    pallas_call x1, Pallas kernels, block_product(): pl.pallas_call(block_kernel, name='block_product', grid_spec=pltpu.Prefet...  23.1 us

profile of v1, /device:TPU:1, one launch (start us, length us, event | category | flops | bytes accessed | tf_op | source)
XLA Modules:
  0.0 197.5 jit_solution(11561543367697960064)
XLA Ops:
  1.3 1.3 reduce.rows_ref
  2.6 1.3 reduce.1.cols_ref
  3.8 63.3 %gather_rows.1.block_hbm = bf16[128,128,256]{2,1,0:T(8,128)(2,1)} custom-call(bf16[16,128,256]{2,1,0:T(8,128)(2,1)} %bitcast.8, bf16[16,128,256]{2,1,0:T(8,128)(2,1)} %bitcast.9), custom_call_target="tpu_custom_call" | custom-call | tf_op jit(solution)/shard_map/gather_rows/pallas_call | solution.py:205
  67.1 23.1 %block_product.1.part_hbm = bf16[256,128,256]{2,1,0:T(8,128)(2,1)} custom-call(s32[320]{0:T(512)} %reduce.rows_ref, s32[320]{0:T(512)} %reduce.1.cols_ref, s32[1]{0:T(128)} %bitcast.6.count_ref, bf16[128,128,256]{2,1,0:T(8,128)(2,1)} %gather_rows.1.block_hbm, bf16[320,128,128]{2,1,0:T(8,128)(2,1)} %bitcast.7), custom_call_target="tpu_custom_call" | custom-call | flops 2684354560 | bytes 35651584 | tf_op jit(solution)/shard_map/block_product/pallas_call | solution.py:101
  90.2 103.3 %reduce_finish.1 = (bf16[16,128,256]{2,1,0:T(8,128)(2,1)}, f32[256,256]{1,0:T(8,128)}) custom-call(bf16[256,128,256]{2,1,0:T(8,128)(2,1)} %block_product.1.part_hbm, bf16[16,128,256]{2,1,0:T(8,128)(2,1)} %bitcast.10, bf16[256,256]{1,0:T(8,128)(2,1)} %weight_ref.1), custom_call_target="tpu_custom_call" | custom-call | tf_op jit(solution)/shard_map/reduce_finish/pallas_call | solution.py:424
  193.6 2.3 %copy.13 = bf16[2048,256]{1,0:T(8,128)(2,1)} copy(bf16[2048,256]{1,0:T(8,128)(2,1)} %bitcast.11) | data formatting | bytes 2097152
  195.8 1.7 copy.14

commit v2 on v0

v2 whole, which is shorter than its diff:
```python
import math

import jax
import jax.numpy as jnp
from jax import lax
from jax.experimental import pallas as pl
from jax.experimental.pallas import tpu as pltpu
from jax.sharding import PartitionSpec as P

MESH = pl.DeviceIdType.MESH
GROUP = 8
LANES = 128
ORDER = tuple((s, d) for s in (0, 1) for d in (2, 1, 3, 0))
GATHER, REDUCE, SUM = 14, 24, 35


def place():
    r, q = lax.axis_index("row"), lax.axis_index("col")
    core, y, z_hi = lax.rem(r, 2), lax.rem(lax.div(r, 2), 4), lax.div(r, 8)
    x, z_lo = lax.rem(q, 4), lax.div(q, 4)
    return core, x, y, z_hi, z_lo


def device(core, x, y, z_hi, z_lo):
    return ((z_hi * 4 + y) * 2 + core, z_lo * 4 + x)


def meet(partners):
    barrier = pltpu.get_barrier_semaphore()
    for partner in partners:
        pl.semaphore_signal(barrier, inc=1, device_id=partner, device_id_type=MESH)
    pl.semaphore_wait(barrier, len(partners))


def layer_kernel(order_ref, last_ref, grad_hbm, preact_hbm, features_hbm, weight_ref, tiles_hbm,
                 grad_out_hbm, gw_ref,
                 tiles, block_0, block_1, runs, mate_part, own, core_in, far_l, far_r, near_l, near_r,
                 relay, cross, features, grads, term, core_half, plane_in, z_in, halves,
                 load_sem, send_sem, recv_sem):
    core, x, y, z_hi, z_lo = place()
    block = (block_0, block_1)
    count = own.shape[1]
    half = count // 2
    slots = tiles.shape[0]
    row_bits = int(math.log2(block_0.shape[0]))
    z = z_hi * 2 + z_lo
    x_r, x_l, x_o = lax.rem(x + 1, 4), lax.rem(x + 3, 4), lax.rem(x + 2, 4)

    def at_z(zz):
        return device(core, x, y, lax.div(zz, 2), lax.rem(zz, 2))

    mate = device(1 - core, x, y, z_hi, z_lo)
    x_right, x_left = device(core, x_r, y, z_hi, z_lo), device(core, x_l, y, z_hi, z_lo)
    over = device(core, x, y, z_hi, 1 - z_lo)
    y_right = device(core, x, lax.rem(y + 1, 4), z_hi, z_lo)
    y_left = device(core, x, lax.rem(y + 3, 4), z_hi, z_lo)
    above, below = at_z(lax.rem(z + 1, 4)), at_z(lax.rem(z + 3, 4))
    plane = [device(core, lax.rem(x + d % 4, 4), lax.rem(y + d // 4, 4), z_hi, z_lo)
             for d in range(1, 16)]
    column = [at_z(lax.rem(z + d, 4)) for d in range(1, 4)]
    sent, done = [], []

    def go(n, source, target_ref, target):
        copy = pltpu.make_async_remote_copy(
            src_ref=source, dst_ref=target_ref, send_sem=send_sem.at[n], recv_sem=recv_sem.at[n],
            device_id=target, device_id_type=MESH)
        copy.start()
        sent.append(copy)
        return copy

    def fetch(n, source, target_ref):
        copy = pltpu.make_async_copy(source, target_ref, load_sem.at[n])
        copy.start()
        return copy

    stages = []
    for h in range(2):
        lanes = pl.ds(h * LANES, LANES)
        stages.append((
            fetch(2 * h, grad_hbm.at[:, :, lanes], runs.at[pl.ds(2 * h * count, count)]),
            fetch(2 * h + 1, preact_hbm.at[:, :, lanes], runs.at[pl.ds((2 * h + 1) * count, count)])))
    quarter = slots // 4
    tile_loads = [fetch(4 + p, tiles_hbm.at[pl.ds(p * quarter, quarter)], tiles.at[pl.ds(p * quarter, quarter)])
                  for p in range(4)]
    feature_load = fetch(8, features_hbm, features)
    mine = (z_lo * 4 + x) * count

    def mask(h):
        for load in stages[h]:
            load.wait()

        def one(t, carry):
            g = runs[2 * h * count + t]
            keep = runs[(2 * h + 1) * count + t].astype(jnp.float32) > 0
            block[h][mine + t] = jnp.where(keep, g.astype(jnp.float32), 0.0).astype(jnp.bfloat16)
            return carry
        lax.fori_loop(0, count, one, 0)

    mask(0)
    meet([mate] + plane + column)

    gathers = ({}, {})

    def pass_on(h, n, z_at, x_at, part, target):
        spot = block[h].at[pl.ds((z_at * 4 + x_at) * count + part * half, half)]
        gathers[h][n] = go(h * GATHER + n, spot, spot, target)

    def gather_first(h):
        pass_on(h, 0, z_lo, x, 0, x_right)
        pass_on(h, 1, z_lo, x, 1, x_left)
        pass_on(h, 2, z_lo, x, 0, over)
        pass_on(h, 4, z_lo, x, 1, x_right)
        pass_on(h, 5, z_lo, x, 0, x_left)
        pass_on(h, 3, z_lo, x, 1, over)

    def gather_second(h):
        gathers[h][0].wait_recv()
        pass_on(h, 6, z_lo, x_l, 0, x_right)
        gathers[h][1].wait_recv()
        pass_on(h, 7, z_lo, x_r, 1, x_left)
        gathers[h][2].wait_recv()
        pass_on(h, 8, 1 - z_lo, x, 0, x_right)
        pass_on(h, 9, 1 - z_lo, x, 0, x_left)
        gathers[h][3].wait_recv()
        pass_on(h, 10, 1 - z_lo, x, 1, x_right)
        pass_on(h, 11, 1 - z_lo, x, 1, x_left)

    def gather_third(h):
        gathers[h][6].wait_recv()
        pass_on(h, 12, z_lo, x_o, 0, over)
        gathers[h][7].wait_recv()
        pass_on(h, 13, z_lo, x_o, 1, over)

    def gather_rest(h):
        for n in (4, 5, 8, 9, 10, 11, 12, 13):
            gathers[h][n].wait_recv()

    def turn(p):
        tile_loads[p].wait()

        def one(i, carry):
            for u in range(4):
                k = p * quarter + i * 4 + u
                tiles[k] = tiles[k].T
            return carry
        lax.fori_loop(0, quarter // 4, one, 0)

    def multiply(h, start, stop, acc):
        def one(g, acc):
            prods, keeps = [], []
            for u in range(GROUP):
                entry = order_ref[g * GROUP + u]
                keeps.append((entry & 1) > 0)
                row = (entry >> 1) & (block_0.shape[0] - 1)
                prods.append(jnp.dot(tiles[entry >> (row_bits + 1)], block[h][row],
                                     preferred_element_type=jnp.float32))
            for u in range(GROUP):
                acc = jnp.where(keeps[u], acc, 0.0) + prods[u]
                runs[g * GROUP + u] = acc.astype(jnp.bfloat16)
            return acc
        return lax.fori_loop(start // GROUP, stop // GROUP, one, acc)

    def chunk(s, d, c):
        z_to = 1 - z_hi if s == 0 else z_hi
        return ((z_to * 4 + lax.rem(y + d, 4)) * 2 + c) * count

    def column_total(c):
        entry = last_ref[c]
        return runs[entry >> 1].astype(jnp.float32) * (entry & 1).astype(jnp.float32)

    swaps = ({}, {})

    def swap(h, n):
        s, d = ORDER[n]
        base = chunk(s, d, 1 - core)

        def one(t, carry):
            mate_part[n, t] = column_total(base + t).astype(jnp.bfloat16)
            return carry
        if h == 1:
            swaps[0][n].wait_send()
            done.append(swaps[0][n])
        lax.fori_loop(0, count, one, 0)
        swaps[h][n] = go(2 * GATHER + h * REDUCE + n, mate_part.at[n], core_in.at[h * 8 + s * 4 + d], mate)

    def settle(h, n):
        if n == 0:
            for m in range(3):
                swap(h, m)
        if n + 3 < len(ORDER):
            swap(h, n + 3)
        s, d = ORDER[n]
        base = chunk(s, d, core)
        at = h * 8 + s * 4 + d
        swaps[h][n].wait_recv()

        def one(t, carry):
            own[at, t] = (column_total(base + t) + core_in[at, t].astype(jnp.float32)).astype(jnp.bfloat16)
            return carry
        lax.fori_loop(0, count, one, 0)

    low, high = pl.ds(0, half), pl.ds(half, half)
    far, direct, merged, hops = {}, {}, {}, {}

    def spread(h, s):
        first, at, b = s * 4, h * 8 + s * 4, h * 2 + s
        base = 2 * GATHER + h * REDUCE + 8 + s * 6
        settle(h, first)
        far[b] = (go(base, own.at[at + 2, low], far_l.at[b], y_right),
                  go(base + 1, own.at[at + 2, high], far_r.at[b], y_left))
        settle(h, first + 1)
        one = go(base + 2, own.at[at + 1, high], near_l.at[b, high], y_right)
        settle(h, first + 2)
        two = go(base + 3, own.at[at + 3, low], near_r.at[b, low], y_left)
        direct[b] = (one, two)
        settle(h, first + 3)

    def add_far(at, start, src, b):
        def one(t, carry):
            own[at, start + t] = (own[at, start + t].astype(jnp.float32)
                                  + src[b, t].astype(jnp.float32)).astype(jnp.bfloat16)
            return carry
        lax.fori_loop(0, half, one, 0)

    def forward(h, s):
        at, b = h * 8 + s * 4, h * 2 + s
        base = 2 * GATHER + h * REDUCE + 8 + s * 6
        far[b][0].wait_recv()
        add_far(at + 1, 0, far_l, b)
        one = go(base + 4, own.at[at + 1, low], near_l.at[b, low], y_right)
        far[b][1].wait_recv()
        add_far(at + 3, half, far_r, b)
        two = go(base + 5, own.at[at + 3, high], near_r.at[b, high], y_left)
        merged[b] = (one, two)

    def near_sum(at, b, t):
        return (own[at, t].astype(jnp.float32) + near_l[b, t].astype(jnp.float32)
                + near_r[b, t].astype(jnp.float32))

    def near_wait(b, part):
        merged[b][part].wait_recv()
        direct[b][1 - part].wait_recv()

    def close(h):
        at, b = h * 8, h * 2
        base = 2 * GATHER + h * REDUCE + 20
        for part in range(2):
            near_wait(b, part)

            def one(t, carry):
                tt = part * half + t
                own[at, tt] = near_sum(at, b, tt).astype(jnp.bfloat16)
                return carry
            lax.fori_loop(0, half, one, 0)
            hops[h, part] = go(base + part, own.at[at, low if part == 0 else high],
                               relay.at[h * 2 + part], above if part == 0 else below)

    def onward(h):
        base = 2 * GATHER + h * REDUCE + 22
        for part in range(2):
            hops[h, part].wait_recv()
            hops[h, 2 + part] = go(base + part, relay.at[h * 2 + part], cross.at[h * 2 + part],
                                   above if part == 0 else below)

    pair = 4

    def total_of(h):
        at, b = h * 8 + 4, h * 2 + 1
        for part in range(2):
            near_wait(b, part)
            hops[h, 2 + part].wait_recv()

            def one(g, acc):
                t = part * half + g * pair
                spot = pl.ds(t, pair)
                summed = (near_sum(at, b, spot)
                          + cross[h * 2 + part, pl.ds(g * pair, pair)].astype(jnp.float32)).astype(jnp.bfloat16)
                own[at, spot] = summed
                summed = summed.reshape(pair * LANES, LANES)
                if h == 1:
                    before = own[4, spot].reshape(pair * LANES, LANES)
                    both = jnp.concatenate([before, summed], axis=1)
                    out = lax.dot_general(both, weight_ref[...], (((1,), (1,)), ((), ())),
                                          preferred_element_type=jnp.float32)
                    grads[spot] = out.astype(jnp.bfloat16).reshape((pair,) + grads.shape[1:])
                feats = features[spot].reshape(pair * LANES, features.shape[2])
                return acc + lax.dot_general(feats, summed, (((0,), (0,)), ((), ())),
                                             preferred_element_type=jnp.float32)
            acc = lax.fori_loop(0, half // pair, one, jnp.zeros((term.shape[0], LANES), jnp.float32))
            if part == 0:
                term[:, h * LANES:(h + 1) * LANES] = acc
            else:
                term[:, h * LANES:(h + 1) * LANES] += acc

    nothing = jnp.zeros((LANES, LANES), jnp.float32)
    middle = slots // 2 // GROUP * GROUP
    gather_first(0)
    mask(1)
    turn(0)
    gather_second(0)
    turn(1)
    turn(2)
    gather_third(0)
    gather_first(1)
    turn(3)
    gather_rest(0)
    acc = multiply(0, 0, middle, nothing)
    gather_second(1)
    multiply(0, middle, slots, acc)
    spread(0, 0)
    gather_third(1)
    forward(0, 0)
    spread(0, 1)
    gather_rest(1)
    acc = multiply(1, 0, middle, nothing)
    close(0)
    multiply(1, middle, slots, acc)
    forward(0, 1)
    spread(1, 0)
    onward(0)
    forward(1, 0)
    spread(1, 1)
    feature_load.wait()
    total_of(0)
    close(1)
    forward(1, 1)
    onward(1)
    total_of(1)
    store = fetch(9, grads, grad_out_hbm)

    first = 2 * GATHER + 2 * REDUCE
    lines = core_half.shape[0]
    piece = lines // 16
    spot = y * 4 + x

    def piece_of(p):
        return pl.ds(pl.multiple_of(p * piece, piece), piece)

    def side_of(c):
        return pl.ds(pl.multiple_of(c * lines, lines), lines)

    trade = go(first, term.at[side_of(1 - core)], core_half, mate)
    trade.wait_recv()
    halves[...] = term[side_of(core), :] + core_half[...]
    spots = [lax.rem(y + d // 4, 4) * 4 + lax.rem(x + d % 4, 4) for d in range(1, 16)]
    out = [go(first + d, halves.at[piece_of(spots[d - 1])], plane_in.at[d - 1], plane[d - 1])
           for d in range(1, 16)]
    total = halves[piece_of(spot), :]
    for d in range(1, 16):
        out[d - 1].wait_recv()
        total = total + plane_in[d - 1]
    z_in[z] = total
    ups = [go(first + 15 + d, z_in.at[z], z_in.at[z], column[d - 1]) for d in range(1, 4)]
    for copy in ups:
        copy.wait_recv()
    total = (z_in[0] + z_in[1]) + (z_in[2] + z_in[3])
    part = pl.ds(pl.multiple_of(core * lines + spot * piece, piece), piece)
    gw_ref[part, :] = total
    out = [go(first + 18 + d, gw_ref.at[part], gw_ref.at[part], plane[d - 1]) for d in range(1, 16)]
    for copy in out:
        copy.wait_recv()
    trade = go(first + 34, gw_ref.at[side_of(core)], gw_ref.at[side_of(core)], mate)
    trade.wait_recv()
    store.wait()
    for copy in sent:
        if not any(copy is one for one in done):
            copy.wait_send()


def layer_backward(order, last, grad_out, preact, features, weight, tiles, members):
    count, side, width = grad_out.shape
    depth = weight.shape[0]
    slots = tiles.shape[0]
    piece = (side, LANES)
    full, part = (count,) + piece, (count // 2,) + piece
    n_sems = 2 * GATHER + 2 * REDUCE + SUM

    def bf16(*shape):
        return pltpu.VMEM(shape, jnp.bfloat16)

    def f32(*shape):
        return pltpu.VMEM(shape, jnp.float32)

    return pl.pallas_call(
        layer_kernel,
        name="layer_backward",
        in_specs=[pl.BlockSpec(memory_space=pltpu.SMEM)] * 2
        + [pl.BlockSpec(memory_space=pl.ANY)] * 3
        + [pl.BlockSpec(memory_space=pltpu.VMEM), pl.BlockSpec(memory_space=pl.ANY)],
        out_specs=[pl.BlockSpec(memory_space=pl.ANY), pl.BlockSpec(memory_space=pltpu.VMEM)],
        out_shape=[jax.ShapeDtypeStruct((count, side, width), jnp.bfloat16),
                   jax.ShapeDtypeStruct((depth, width), jnp.float32)],
        scratch_shapes=[
            bf16(slots, *piece),
            bf16(members * count, *piece),
            bf16(members * count, *piece),
            bf16(slots, *piece),
            bf16(8, *full),
            bf16(16, *full),
            bf16(16, *full),
            bf16(4, *part),
            bf16(4, *part),
            bf16(4, *full),
            bf16(4, *full),
            bf16(4, *part),
            bf16(4, *part),
            bf16(count, side, width),
            bf16(count, side, width),
            f32(depth, width),
            f32(depth // 2, width),
            f32(15, depth // 32, width),
            f32(4, depth // 32, width),
            f32(depth // 2, width),
            pltpu.SemaphoreType.DMA((10,)),
            pltpu.SemaphoreType.DMA((n_sems,)),
            pltpu.SemaphoreType.DMA((n_sems,)),
        ],
        compiler_params=pltpu.CompilerParams(
            collective_id=0, has_side_effects=True, vmem_limit_bytes=63 * 1024 * 1024),
    )(order, last, grad_out, preact, features, weight, tiles)


def slot_tables(rows, cols, live_count, row_tiles, col_tiles):
    slots = rows.shape[0]
    k = lax.iota(jnp.int32, slots)
    live = k < live_count
    col = jnp.where(live, cols, col_tiles)
    key = col * slots + k
    rank = jnp.sum((key[None, :] < key[:, None]).astype(jnp.int32), axis=1)
    same = (col[None, :] == col[:, None]) & (k[None, :] < k[:, None])
    again = jnp.max(same.astype(jnp.int32), axis=1)
    packed = (k * row_tiles + rows) * 2 + again
    order = jnp.sum(jnp.where(rank[None, :] == k[:, None], packed[None, :], 0), axis=1)
    c = lax.iota(jnp.int32, col_tiles)
    upto = jnp.sum((col[None, :] <= c[:, None]).astype(jnp.int32), axis=1)
    here = jnp.max((col[None, :] == c[:, None]).astype(jnp.int32), axis=1)
    last = jnp.maximum(upto - 1, 0) * 2 + here
    return order, last


def body(grad_out, preact, features, weight, tiles, tile_rows, tile_cols, live_counts):
    nodes, width = grad_out.shape
    side = tiles.shape[-1]
    slots = tiles.shape[2]
    shape = (nodes // side, side, width)
    members = lax.axis_size("col")
    col_tiles = lax.axis_size("row") * nodes // side
    order, last = slot_tables(
        tile_rows.reshape(slots), tile_cols.reshape(slots), live_counts.reshape(()),
        members * nodes // side, col_tiles)
    grad_features, grad_weight = layer_backward(
        order, last, grad_out.reshape(shape), preact.reshape(shape), features.reshape(shape), weight,
        tiles.reshape(slots, side, side), members)
    return (grad_features.reshape(nodes, width), grad_weight)


def solution(mesh):
    in_specs = (
        P(("row", "col"), None),
        P(("row", "col"), None),
        P(("col", "row"), None),
        P(),
        P("row", "col", None, None, None),
        P("row", "col", None),
        P("row", "col", None),
        P("row", "col"),
    )
    out_specs = (P(("col", "row"), None), P())
    return jax.shard_map(body, mesh=mesh, in_specs=in_specs, out_specs=out_specs, check_vma=False)
```

time: 806 us -> 158 us (0.20)
  waiting for transfers between devices: 367 us -> 0 us
  matrix products: 304 us -> 0 us
  Pallas kernels: 0 us -> 149 us
  local copies, waits for them, and re-layouts: 87.5 us -> 3.93 us
  other arithmetic: 30.8 us -> 3.18 us
  between operations: 13.8 us -> 1.3 us
    dot_general x32 -> x0, matrix products: 304 us -> none  [the longest x10 234 us: add_group(): jnp.dot(both_place, both_vals, preferred_element_type=jnp.float32)]
    pallas_call x0 -> x1, Pallas kernels: none -> 149 us  [layer_backward(): pl.pallas_call(layer_kernel, name='layer_backward', in_specs=[pl.BlockSpe...]
    reduce_scatter x1 -> x0, waiting for transfers between devices: 145 us -> none  [body(): lax.psum_scatter(partial_value.astype(jnp.bfloat16), 'row', scatter_dimen...]
    psum x1 -> x0, waiting for transfers between devices: 141 us -> none  [body(): grad_weight = lax.psum(weight_term, ('row', 'col'))]
    all_gather x1 -> x0, waiting for transfers between devices: 80.9 us -> none  [body(): block = lax.all_gather(masked, 'col', axis=0, tiled=True)]
    while x20 -> x0, local copies, waits for them, and re-layouts: 30.6 us -> none
    convert_element_type x1 -> x0, local copies, waits for them, and re-layouts: 25.6 us -> none  [body(): partial_value.astype(jnp.bfloat16)]
    convert_element_type x1 -> x0, other arithmetic: 17.1 us -> none  [body(): partial_value.astype(jnp.bfloat16)]
  transfers between devices with their start and end apart: 3 -> 0, of which waited for: 3 -> 0; matrix products, arithmetic and copies ran while one was open for 2% -> 0% of each run, Pallas kernels for 0% -> 0%
where the time goes in v2:
time: 158 us
  Pallas kernels  149 us (94%)
  local copies, waits for them, and re-layouts  3.93 us (2%)
  other arithmetic  3.18 us (2%)
    pallas_call x1, Pallas kernels, layer_backward(): pl.pallas_call(layer_kernel, name='layer_backward', in_specs=[pl.BlockSpe...  149 us
    unnamed x2, local copies, waits for them, and re-layouts  3.93 us

profile of v2, /device:TPU:1, one launch (start us, length us, event | category | flops | bytes accessed | tf_op | source)
XLA Modules:
  0.0 157.7 jit_solution(8554219260545932305)
XLA Ops:
  1.3 0.7 reduce.1
  2.0 0.7 reduce
  2.7 0.3 convert_reduce_fusion
  3.0 0.7 select_reduce_fusion.order_ref
  3.7 0.2 convert_reduce_fusion.3
  3.9 0.6 multiply_add_fusion.1.last_ref
  4.5 149.3 %layer_backward.1 = (bf16[16,128,256]{2,1,0:T(8,128)(2,1)}, f32[256,256]{1,0:T(8,128)}) custom-call(s32[320]{0:T(512)} %select_reduce_fusion.order_ref, s32[256]{0:T(256)} %multiply_add_fusion.1.last_ref, bf16[16,128,256]{2,1,0:T(8,128)(2,1)} %bitcast.8, bf16[16,128,256]{2,1,0:T(8,128)(2,1)} %bitcast.9, bf16[16,128,256]{2,1,0:T(8,128)(2,1)} %bitcast.10, ...), custom_call_target="tpu_custom_call" | custom-call | tf_op jit(solution)/shard_map/layer_backward/pallas_call | solution.py:384
  153.8 2.3 %copy.13 = bf16[2048,256]{1,0:T(8,128)(2,1)} copy(bf16[2048,256]{1,0:T(8,128)(2,1)} %bitcast.11) | data formatting | bytes 2097152
  156.1 1.7 %copy.14 = f32[256,256]{1,0:T(8,128)} copy(f32[256,256]{1,0:T(8,128)} %get-tuple-element.15) | data formatting | bytes 524288
  (2 shorter events, 0.0 us)

commit v3 on v2

--- a/solution.py
+++ b/solution.py
@@ -8,10 +8,11 @@
 from jax.sharding import PartitionSpec as P
 
 MESH = pl.DeviceIdType.MESH
-GROUP = 8
+GROUP = 16
 LANES = 128
 ORDER = tuple((s, d) for s in (0, 1) for d in (2, 1, 3, 0))
-GATHER, REDUCE, SUM = 14, 24, 35
+GATHER, REDUCE, SUM = 14, 34, 35
+FIRST = (2, 6)
 
 
 def place():
@@ -35,7 +36,7 @@
 def layer_kernel(order_ref, last_ref, grad_hbm, preact_hbm, features_hbm, weight_ref, tiles_hbm,
                  grad_out_hbm, gw_ref,
                  tiles, block_0, block_1, runs, mate_part, own, core_in, far_l, far_r, near_l, near_r,
-                 relay, cross, features, grads, term, core_half, plane_in, z_in, halves,
+                 relay, cross, early_0, early_1, early_in_0, early_in_1, features, terms, term, core_half, plane_in, z_in, halves,
                  load_sem, send_sem, recv_sem):
     core, x, y, z_hi, z_lo = place()
     block = (block_0, block_1)
@@ -59,6 +60,7 @@
              for d in range(1, 16)]
     column = [at_z(lax.rem(z + d, 4)) for d in range(1, 4)]
     sent, done = [], []
+    early, early_in = (early_0, early_1), (early_in_0, early_in_1)
 
     def go(n, source, target_ref, target):
         copy = pltpu.make_async_remote_copy(
@@ -96,8 +98,8 @@
             return carry
         lax.fori_loop(0, count, one, 0)
 
+    meet([mate] + plane + column)
     mask(0)
-    meet([mate] + plane + column)
 
     gathers = ({}, {})
 
@@ -139,11 +141,11 @@
         tile_loads[p].wait()
 
         def one(i, carry):
-            for u in range(4):
-                k = p * quarter + i * 4 + u
+            for u in range(8):
+                k = p * quarter + i * 8 + u
                 tiles[k] = tiles[k].T
             return carry
-        lax.fori_loop(0, quarter // 4, one, 0)
+        lax.fori_loop(0, quarter // 8, one, 0)
 
     def multiply(h, start, stop, acc):
         def one(g, acc):
@@ -164,23 +166,23 @@
         z_to = 1 - z_hi if s == 0 else z_hi
         return ((z_to * 4 + lax.rem(y + d, 4)) * 2 + c) * count
 
-    def column_total(c):
-        entry = last_ref[c]
-        return runs[entry >> 1].astype(jnp.float32) * (entry & 1).astype(jnp.float32)
-
+    zero = jnp.zeros((LANES, LANES), jnp.bfloat16)
     swaps = ({}, {})
 
     def swap(h, n):
         s, d = ORDER[n]
         base = chunk(s, d, 1 - core)
 
-        def one(t, carry):
-            mate_part[n, t] = column_total(base + t).astype(jnp.bfloat16)
+        def one(g, carry):
+            for u in range(8):
+                t = g * 8 + u
+                entry = last_ref[base + t]
+                mate_part[n, t] = jnp.where((entry & 1) > 0, runs[entry >> 1], zero)
             return carry
         if h == 1:
             swaps[0][n].wait_send()
             done.append(swaps[0][n])
-        lax.fori_loop(0, count, one, 0)
+        lax.fori_loop(0, count // 8, one, 0)
         swaps[h][n] = go(2 * GATHER + h * REDUCE + n, mate_part.at[n], core_in.at[h * 8 + s * 4 + d], mate)
 
     def settle(h, n):
@@ -194,103 +196,145 @@
         at = h * 8 + s * 4 + d
         swaps[h][n].wait_recv()
 
-        def one(t, carry):
-            own[at, t] = (column_total(base + t) + core_in[at, t].astype(jnp.float32)).astype(jnp.bfloat16)
+        def one(g, carry):
+            for u in range(8):
+                t = g * 8 + u
+                entry = last_ref[base + t]
+                mine_here = jnp.where((entry & 1) > 0, runs[entry >> 1], zero).astype(jnp.float32)
+                own[at, t] = (mine_here + core_in[at, t].astype(jnp.float32)).astype(jnp.bfloat16)
             return carry
-        lax.fori_loop(0, count, one, 0)
-
-    low, high = pl.ds(0, half), pl.ds(half, half)
+        lax.fori_loop(0, count // 8, one, 0)
+
     far, direct, merged, hops = {}, {}, {}, {}
 
-    def spread(h, s):
-        first, at, b = s * 4, h * 8 + s * 4, h * 2 + s
-        base = 2 * GATHER + h * REDUCE + 8 + s * 6
-        settle(h, first)
-        far[b] = (go(base, own.at[at + 2, low], far_l.at[b], y_right),
-                  go(base + 1, own.at[at + 2, high], far_r.at[b], y_left))
-        settle(h, first + 1)
+    def base_of(h):
+        return 2 * GATHER + h * REDUCE + 8
+
+    def segment(h, g):
+        rest = count - FIRST[h]
+        s, start, length = ((0, 0, rest), (1, 0, rest), (1, rest, FIRST[h]))[g]
+        return s, start, length // 2, h * 8 + s * 4, h * 2 + s
+
+    def spread(h, g):
+        s, start, size, at, b = segment(h, g)
+        base = base_of(h) + g * 6
+        low, high = pl.ds(start, size), pl.ds(start + size, size)
+        spot = pl.ds(start // 2, size)
+        if g < 2:
+            settle(h, s * 4)
+        far[h, g] = (go(base, own.at[at + 2, low], far_l.at[b, spot], y_right),
+                     go(base + 1, own.at[at + 2, high], far_r.at[b, spot], y_left))
+        if g < 2:
+            settle(h, s * 4 + 1)
         one = go(base + 2, own.at[at + 1, high], near_l.at[b, high], y_right)
-        settle(h, first + 2)
+        if g < 2:
+            settle(h, s * 4 + 2)
         two = go(base + 3, own.at[at + 3, low], near_r.at[b, low], y_left)
-        direct[b] = (one, two)
-        settle(h, first + 3)
-
-    def add_far(at, start, src, b):
-        def one(t, carry):
+        direct[h, g] = (one, two)
+        if g < 2:
+            settle(h, s * 4 + 3)
+
+    def add_far(at, start, size, src, b, spot):
+        for t in range(size):
             own[at, start + t] = (own[at, start + t].astype(jnp.float32)
-                                  + src[b, t].astype(jnp.float32)).astype(jnp.bfloat16)
-            return carry
-        lax.fori_loop(0, half, one, 0)
-
-    def forward(h, s):
-        at, b = h * 8 + s * 4, h * 2 + s
-        base = 2 * GATHER + h * REDUCE + 8 + s * 6
-        far[b][0].wait_recv()
-        add_far(at + 1, 0, far_l, b)
+                                  + src[b, spot + t].astype(jnp.float32)).astype(jnp.bfloat16)
+
+    def forward(h, g):
+        s, start, size, at, b = segment(h, g)
+        base = base_of(h) + g * 6
+        low, high = pl.ds(start, size), pl.ds(start + size, size)
+        far[h, g][0].wait_recv()
+        add_far(at + 1, start, size, far_l, b, start // 2)
         one = go(base + 4, own.at[at + 1, low], near_l.at[b, low], y_right)
-        far[b][1].wait_recv()
-        add_far(at + 3, half, far_r, b)
+        far[h, g][1].wait_recv()
+        add_far(at + 3, start + size, size, far_r, b, start // 2)
         two = go(base + 5, own.at[at + 3, high], near_r.at[b, high], y_left)
-        merged[b] = (one, two)
+        merged[h, g] = (one, two)
 
     def near_sum(at, b, t):
         return (own[at, t].astype(jnp.float32) + near_l[b, t].astype(jnp.float32)
                 + near_r[b, t].astype(jnp.float32))
 
-    def near_wait(b, part):
-        merged[b][part].wait_recv()
-        direct[b][1 - part].wait_recv()
+    def near_wait(h, g, part):
+        merged[h, g][part].wait_recv()
+        direct[h, g][1 - part].wait_recv()
+
+    def early_send(h):
+        size = FIRST[h] // 2
+        for part in range(2):
+            rows = pl.ds(count - FIRST[h] + part * size, size)
+            hops[h, 4 + part] = go(base_of(h) + 22 + part, own.at[pl.ds(h * 8, 4), rows],
+                                   early[h].at[part], below if part else above)
+
+    def early_hop(h):
+        for part in range(2):
+            hops[h, 4 + part].wait_recv()
+            hops[h, 6 + part] = go(base_of(h) + 24 + part, early[h].at[part],
+                                   early_in[h].at[part], below if part else above)
+
+    def early_add(h):
+        size = FIRST[h] // 2
+        for part in range(2):
+            hops[h, 6 + part].wait_recv()
+            for d in range(4):
+                for t in range(size):
+                    tt = count - FIRST[h] + part * size + t
+                    own[h * 8 + 4 + d, tt] = (
+                        own[h * 8 + 4 + d, tt].astype(jnp.float32)
+                        + early_in[h][part, d, t].astype(jnp.float32)).astype(jnp.bfloat16)
 
     def close(h):
-        at, b = h * 8, h * 2
-        base = 2 * GATHER + h * REDUCE + 20
+        s, start, size, at, b = segment(h, 0)
         for part in range(2):
-            near_wait(b, part)
-
-            def one(t, carry):
-                tt = part * half + t
-                own[at, tt] = near_sum(at, b, tt).astype(jnp.bfloat16)
-                return carry
-            lax.fori_loop(0, half, one, 0)
-            hops[h, part] = go(base + part, own.at[at, low if part == 0 else high],
-                               relay.at[h * 2 + part], above if part == 0 else below)
+            near_wait(h, 0, part)
+
+            for t in range(part * size, (part + 1) * size):
+                own[at, t] = near_sum(at, b, t).astype(jnp.bfloat16)
+            hops[h, part] = go(base_of(h) + 18 + part, own.at[at, pl.ds(part * size, size)],
+                               relay.at[h * 2 + part, pl.ds(0, size)], below if part else above)
 
     def onward(h):
-        base = 2 * GATHER + h * REDUCE + 22
+        size = segment(h, 0)[2]
         for part in range(2):
             hops[h, part].wait_recv()
-            hops[h, 2 + part] = go(base + part, relay.at[h * 2 + part], cross.at[h * 2 + part],
-                                   above if part == 0 else below)
+            spot = pl.ds(0, size)
+            hops[h, 2 + part] = go(base_of(h) + 20 + part, relay.at[h * 2 + part, spot],
+                                   cross.at[h * 2 + part, spot], below if part else above)
+
+    def total_of(h, g):
+        s, start, size, at, b = segment(h, g)
+        for part in range(2):
+            near_wait(h, g, part)
+            spot = pl.ds(start + part * size, size)
+            total = near_sum(at, b, spot)
+            if g == 1:
+                hops[h, 2 + part].wait_recv()
+                total = total + cross[h * 2 + part, pl.ds(0, size)].astype(jnp.float32)
+            summed = total.astype(jnp.bfloat16)
+            own[at, spot] = summed
+            feats = features[spot].reshape(size * LANES, features.shape[2])
+            more = lax.dot_general(feats, summed.reshape(size * LANES, LANES), (((0,), (0,)), ((), ())),
+                                   preferred_element_type=jnp.float32)
+            column = slice(h * LANES, (h + 1) * LANES)
+            held = terms if g == 1 else term
+            if part == 0:
+                held[:, column] = more
+            else:
+                held[:, column] += more
 
     pair = 4
 
-    def total_of(h):
-        at, b = h * 8 + 4, h * 2 + 1
-        for part in range(2):
-            near_wait(b, part)
-            hops[h, 2 + part].wait_recv()
-
-            def one(g, acc):
-                t = part * half + g * pair
-                spot = pl.ds(t, pair)
-                summed = (near_sum(at, b, spot)
-                          + cross[h * 2 + part, pl.ds(g * pair, pair)].astype(jnp.float32)).astype(jnp.bfloat16)
-                own[at, spot] = summed
-                summed = summed.reshape(pair * LANES, LANES)
-                if h == 1:
-                    before = own[4, spot].reshape(pair * LANES, LANES)
-                    both = jnp.concatenate([before, summed], axis=1)
-                    out = lax.dot_general(both, weight_ref[...], (((1,), (1,)), ((), ())),
-                                          preferred_element_type=jnp.float32)
-                    grads[spot] = out.astype(jnp.bfloat16).reshape((pair,) + grads.shape[1:])
-                feats = features[spot].reshape(pair * LANES, features.shape[2])
-                return acc + lax.dot_general(feats, summed, (((0,), (0,)), ((), ())),
-                                             preferred_element_type=jnp.float32)
-            acc = lax.fori_loop(0, half // pair, one, jnp.zeros((term.shape[0], LANES), jnp.float32))
-            if part == 0:
-                term[:, h * LANES:(h + 1) * LANES] = acc
-            else:
-                term[:, h * LANES:(h + 1) * LANES] += acc
+    def feature_grads():
+        def one(g, carry):
+            spot = pl.ds(g * pair, pair)
+            both = jnp.concatenate([own[4, spot].reshape(pair * LANES, LANES),
+                                    own[12, spot].reshape(pair * LANES, LANES)], axis=1)
+            out = lax.dot_general(both, weight_ref[...], (((1,), (1,)), ((), ())),
+                                  preferred_element_type=jnp.float32)
+            features[spot] = out.astype(jnp.bfloat16).reshape((pair,) + features.shape[1:])
+            return carry
+        lax.fori_loop(0, count // pair, one, 0)
+        return fetch(9, features, grad_out_hbm)
 
     nothing = jnp.zeros((LANES, LANES), jnp.float32)
     middle = slots // 2 // GROUP * GROUP
@@ -308,25 +352,36 @@
     gather_second(1)
     multiply(0, middle, slots, acc)
     spread(0, 0)
+    early_send(0)
+    early_hop(0)
     gather_third(1)
     forward(0, 0)
     spread(0, 1)
+    early_add(0)
+    spread(0, 2)
     gather_rest(1)
-    acc = multiply(1, 0, middle, nothing)
     close(0)
-    multiply(1, middle, slots, acc)
     forward(0, 1)
+    multiply(1, 0, slots, nothing)
+    onward(0)
     spread(1, 0)
-    onward(0)
+    early_send(1)
+    forward(0, 2)
     forward(1, 0)
     spread(1, 1)
+    early_hop(1)
     feature_load.wait()
-    total_of(0)
+    total_of(0, 2)
     close(1)
+    total_of(0, 1)
     forward(1, 1)
+    early_add(1)
+    spread(1, 2)
     onward(1)
-    total_of(1)
-    store = fetch(9, grads, grad_out_hbm)
+    forward(1, 2)
+    total_of(1, 1)
+    total_of(1, 2)
+    term[...] = terms[...] + term[...]
 
     first = 2 * GATHER + 2 * REDUCE
     lines = core_half.shape[0]
@@ -340,6 +395,7 @@
         return pl.ds(pl.multiple_of(c * lines, lines), lines)
 
     trade = go(first, term.at[side_of(1 - core)], core_half, mate)
+    store = feature_grads()
     trade.wait_recv()
     halves[...] = term[side_of(core), :] + core_half[...]
     spots = [lax.rem(y + d // 4, 4) * 4 + lax.rem(x + d % 4, 4) for d in range(1, 16)]
@@ -404,8 +460,9 @@
             bf16(4, *full),
             bf16(4, *part),
             bf16(4, *part),
+            *[bf16(2, 4, rows // 2, *piece) for rows in FIRST * 2],
             bf16(count, side, width),
-            bf16(count, side, width),
+            f32(depth, width),
             f32(depth, width),
             f32(depth // 2, width),
             f32(15, depth // 32, width),

time: 158 us -> 149 us (0.943)
  Pallas kernels: 149 us -> 141 us
    pallas_call x1, Pallas kernels: 149 us -> 141 us  [layer_backward(): pl.pallas_call(layer_kernel, name='layer_backward', in_specs=[pl.BlockSpe...]
where the time goes in v3:
time: 149 us
  Pallas kernels  141 us (95%)
  local copies, waits for them, and re-layouts  3.93 us (3%)
  other arithmetic  3.18 us (2%)
    pallas_call x1, Pallas kernels, layer_backward(): pl.pallas_call(layer_kernel, name='layer_backward', in_specs=[pl.BlockSpe...  141 us
    unnamed x2, local copies, waits for them, and re-layouts  3.93 us

profile of v3, /device:TPU:1, one launch (start us, length us, event | category | flops | bytes accessed | tf_op | source)
XLA Modules:
  0.0 148.9 jit_solution(7810162475837321465)
XLA Ops:
  1.3 0.7 reduce.1
  2.0 0.7 reduce
  2.7 0.3 convert_reduce_fusion
  3.0 0.7 select_reduce_fusion.order_ref
  3.7 0.2 convert_reduce_fusion.3
  3.9 0.6 multiply_add_fusion.1.last_ref
  4.5 140.5 %layer_backward.1 = (bf16[16,128,256]{2,1,0:T(8,128)(2,1)}, f32[256,256]{1,0:T(8,128)}) custom-call(s32[320]{0:T(512)} %select_reduce_fusion.order_ref, s32[256]{0:T(256)} %multiply_add_fusion.1.last_ref, bf16[16,128,256]{2,1,0:T(8,128)(2,1)} %bitcast.8, bf16[16,128,256]{2,1,0:T(8,128)(2,1)} %bitcast.9, bf16[16,128,256]{2,1,0:T(8,128)(2,1)} %bitcast.10, ...), custom_call_target="tpu_custom_call" | custom-call | tf_op jit(solution)/shard_map/layer_backward/pallas_call | solution.py:440
  145.0 2.3 %copy.13 = bf16[2048,256]{1,0:T(8,128)(2,1)} copy(bf16[2048,256]{1,0:T(8,128)(2,1)} %bitcast.11) | data formatting | bytes 2097152
  147.2 1.7 %copy.14 = f32[256,256]{1,0:T(8,128)} copy(f32[256,256]{1,0:T(8,128)} %get-tuple-element.15) | data formatting | bytes 524288
  (2 shorter events, 0.0 us)

commit v4 on v3

--- a/solution.py
+++ b/solution.py
@@ -8,10 +8,10 @@
 from jax.sharding import PartitionSpec as P
 
 MESH = pl.DeviceIdType.MESH
-GROUP = 16
+GROUP = 32
 LANES = 128
 ORDER = tuple((s, d) for s in (0, 1) for d in (2, 1, 3, 0))
-GATHER, REDUCE, SUM = 14, 34, 35
+GATHER, REDUCE, SUM = 14, 34, 38
 FIRST = (2, 6)
 
 
@@ -36,7 +36,7 @@
 def layer_kernel(order_ref, last_ref, grad_hbm, preact_hbm, features_hbm, weight_ref, tiles_hbm,
                  grad_out_hbm, gw_ref,
                  tiles, block_0, block_1, runs, mate_part, own, core_in, far_l, far_r, near_l, near_r,
-                 relay, cross, early_0, early_1, early_in_0, early_in_1, features, terms, term, core_half, plane_in, z_in, halves,
+                 relay, cross, early_0, early_1, early_in_0, early_in_1, features, terms, term, plane_in, z_in,
                  load_sem, send_sem, recv_sem):
     core, x, y, z_hi, z_lo = place()
     block = (block_0, block_1)
@@ -58,7 +58,9 @@
     above, below = at_z(lax.rem(z + 1, 4)), at_z(lax.rem(z + 3, 4))
     plane = [device(core, lax.rem(x + d % 4, 4), lax.rem(y + d // 4, 4), z_hi, z_lo)
              for d in range(1, 16)]
-    column = [at_z(lax.rem(z + d, 4)) for d in range(1, 4)]
+    column = [device(core if d % 2 == 0 else 1 - core, x, y,
+                     lax.div(lax.rem(z + d // 2, 4), 2), lax.rem(lax.rem(z + d // 2, 4), 2))
+              for d in range(1, 8)]
     sent, done = [], []
     early, early_in = (early_0, early_1), (early_in_0, early_in_1)
 
@@ -98,7 +100,7 @@
             return carry
         lax.fori_loop(0, count, one, 0)
 
-    meet([mate] + plane + column)
+    meet(plane + column)
     mask(0)
 
     gathers = ({}, {})
@@ -107,13 +109,15 @@
         spot = block[h].at[pl.ds((z_at * 4 + x_at) * count + part * half, half)]
         gathers[h][n] = go(h * GATHER + n, spot, spot, target)
 
-    def gather_first(h):
+    def gather_over(h):
+        pass_on(h, 2, z_lo, x, 0, over)
+        pass_on(h, 3, z_lo, x, 1, over)
+
+    def gather_ring(h):
         pass_on(h, 0, z_lo, x, 0, x_right)
         pass_on(h, 1, z_lo, x, 1, x_left)
-        pass_on(h, 2, z_lo, x, 0, over)
         pass_on(h, 4, z_lo, x, 1, x_right)
         pass_on(h, 5, z_lo, x, 0, x_left)
-        pass_on(h, 3, z_lo, x, 1, over)
 
     def gather_second(h):
         gathers[h][0].wait_recv()
@@ -133,8 +137,12 @@
         gathers[h][7].wait_recv()
         pass_on(h, 13, z_lo, x_o, 1, over)
 
+    def gather_near(h):
+        for n in (4, 5, 8, 9):
+            gathers[h][n].wait_recv()
+
     def gather_rest(h):
-        for n in (4, 5, 8, 9, 10, 11, 12, 13):
+        for n in (10, 11, 12, 13):
             gathers[h][n].wait_recv()
 
     def turn(p):
@@ -338,15 +346,18 @@
 
     nothing = jnp.zeros((LANES, LANES), jnp.float32)
     middle = slots // 2 // GROUP * GROUP
-    gather_first(0)
+    gather_ring(0)
+    gather_over(0)
     mask(1)
     turn(0)
     gather_second(0)
     turn(1)
     turn(2)
     gather_third(0)
-    gather_first(1)
+    gather_over(1)
     turn(3)
+    gather_near(0)
+    gather_ring(1)
     gather_rest(0)
     acc = multiply(0, 0, middle, nothing)
     gather_second(1)
@@ -359,6 +370,7 @@
     spread(0, 1)
     early_add(0)
     spread(0, 2)
+    gather_near(1)
     gather_rest(1)
     close(0)
     forward(0, 1)
@@ -384,39 +396,32 @@
     term[...] = terms[...] + term[...]
 
     first = 2 * GATHER + 2 * REDUCE
-    lines = core_half.shape[0]
-    piece = lines // 16
+    piece = term.shape[0] // 16
     spot = y * 4 + x
 
     def piece_of(p):
         return pl.ds(pl.multiple_of(p * piece, piece), piece)
 
-    def side_of(c):
-        return pl.ds(pl.multiple_of(c * lines, lines), lines)
-
-    trade = go(first, term.at[side_of(1 - core)], core_half, mate)
+    spots = [lax.rem(y + d // 4, 4) * 4 + lax.rem(x + d % 4, 4) for d in range(1, 16)]
+    out = [go(first + d, term.at[piece_of(spots[d - 1])], plane_in.at[d - 1], plane[d - 1])
+           for d in range(1, 16)]
     store = feature_grads()
-    trade.wait_recv()
-    halves[...] = term[side_of(core), :] + core_half[...]
-    spots = [lax.rem(y + d // 4, 4) * 4 + lax.rem(x + d % 4, 4) for d in range(1, 16)]
-    out = [go(first + d, halves.at[piece_of(spots[d - 1])], plane_in.at[d - 1], plane[d - 1])
-           for d in range(1, 16)]
-    total = halves[piece_of(spot), :]
+    total = term[piece_of(spot), :]
     for d in range(1, 16):
         out[d - 1].wait_recv()
         total = total + plane_in[d - 1]
-    z_in[z] = total
-    ups = [go(first + 15 + d, z_in.at[z], z_in.at[z], column[d - 1]) for d in range(1, 4)]
+    me = z * 2 + core
+    z_in[me] = total
+    ups = [go(first + 15 + d, z_in.at[me], z_in.at[me], column[d - 1]) for d in range(1, 8)]
     for copy in ups:
         copy.wait_recv()
-    total = (z_in[0] + z_in[1]) + (z_in[2] + z_in[3])
-    part = pl.ds(pl.multiple_of(core * lines + spot * piece, piece), piece)
+    total = (((z_in[0] + z_in[1]) + (z_in[2] + z_in[3]))
+             + ((z_in[4] + z_in[5]) + (z_in[6] + z_in[7])))
+    part = piece_of(spot)
     gw_ref[part, :] = total
-    out = [go(first + 18 + d, gw_ref.at[part], gw_ref.at[part], plane[d - 1]) for d in range(1, 16)]
+    out = [go(first + 22 + d, gw_ref.at[part], gw_ref.at[part], plane[d - 1]) for d in range(1, 16)]
     for copy in out:
         copy.wait_recv()
-    trade = go(first + 34, gw_ref.at[side_of(core)], gw_ref.at[side_of(core)], mate)
-    trade.wait_recv()
     store.wait()
     for copy in sent:
         if not any(copy is one for one in done):
@@ -464,10 +469,8 @@
             bf16(count, side, width),
             f32(depth, width),
             f32(depth, width),
-            f32(depth // 2, width),
-            f32(15, depth // 32, width),
-            f32(4, depth // 32, width),
-            f32(depth // 2, width),
+            f32(15, depth // 16, width),
+            f32(8, depth // 16, width),
             pltpu.SemaphoreType.DMA((10,)),
             pltpu.SemaphoreType.DMA((n_sems,)),
             pltpu.SemaphoreType.DMA((n_sems,)),
@@ -475,6 +478,21 @@
         compiler_params=pltpu.CompilerParams(
             collective_id=0, has_side_effects=True, vmem_limit_bytes=63 * 1024 * 1024),
     )(order, last, grad_out, preact, features, weight, tiles)
+
+
+def result_kernel(a_in, b_in, a_out, b_out):
+    a_out[...] = a_in[...]
+    b_out[...] = b_in[...]
+
+
+def results(*arrays):
+    return pl.pallas_call(
+        result_kernel,
+        name="results",
+        in_specs=[pl.BlockSpec(memory_space=pltpu.VMEM)] * 2,
+        out_specs=[pl.BlockSpec(memory_space=pltpu.VMEM)] * 2,
+        out_shape=[jax.ShapeDtypeStruct(a.shape, a.dtype) for a in arrays],
+    )(*arrays)
 
 
 def slot_tables(rows, cols, live_count, row_tiles, col_tiles):
@@ -508,7 +526,7 @@
     grad_features, grad_weight = layer_backward(
         order, last, grad_out.reshape(shape), preact.reshape(shape), features.reshape(shape), weight,
         tiles.reshape(slots, side, side), members)
-    return (grad_features.reshape(nodes, width), grad_weight)
+    return tuple(results(grad_features.reshape(nodes, width), grad_weight))
 
 
 def solution(mesh):

time: 149 us -> 147 us (0.987)
  local copies, waits for them, and re-layouts: 3.93 us -> 0 us
    unnamed x2 -> x0, local copies, waits for them, and re-layouts: 3.93 us -> none
    pallas_call x0 -> x1, Pallas kernels: none -> 2.38 us  [results(): pl.pallas_call(result_kernel, name='results', in_specs=[pl.BlockSpec(memo...]
where the time goes in v4:
time: 147 us
  Pallas kernels  142 us (97%)
  other arithmetic  3.18 us (2%)
    pallas_call x1, Pallas kernels, layer_backward(): pl.pallas_call(layer_kernel, name='layer_backward', in_specs=[pl.BlockSpe...  140 us

profile of v4, /device:TPU:1, one launch (start us, length us, event | category | flops | bytes accessed | tf_op | source)
XLA Modules:
  0.0 146.6 jit_solution(14909762645365228240)
XLA Ops:
  1.3 0.7 reduce.1
  2.0 0.7 reduce
  2.7 0.3 convert_reduce_fusion
  3.0 0.7 select_reduce_fusion.order_ref
  3.7 0.2 convert_reduce_fusion.3
  3.9 0.6 multiply_add_fusion.1.last_ref
  4.5 139.7 %layer_backward.1 = (bf16[16,128,256]{2,1,0:T(8,128)(2,1)}, f32[256,256]{1,0:T(8,128)}) custom-call(s32[320]{0:T(512)} %select_reduce_fusion.order_ref, s32[256]{0:T(256)} %multiply_add_fusion.1.last_ref, bf16[16,128,256]{2,1,0:T(8,128)(2,1)} %bitcast.8, bf16[16,128,256]{2,1,0:T(8,128)(2,1)} %bitcast.9, bf16[16,128,256]{2,1,0:T(8,128)(2,1)} %bitcast.10, ...), custom_call_target="tpu_custom_call" | custom-call | tf_op jit(solution)/shard_map/layer_backward/pallas_call | solution.py:445
  144.2 2.4 %results.1 = (bf16[2048,256]{1,0:T(8,128)(2,1)}, f32[256,256]{1,0:T(8,128)}) custom-call(bf16[2048,256]{1,0:T(8,128)(2,1)} %bitcast.11, f32[256,256]{1,0:T(8,128)} %get-tuple-element.5.b_in), custom_call_target="tpu_custom_call" | custom-call | tf_op jit(solution)/shard_map/results/pallas_call | solution.py:489
  (2 shorter events, 0.0 us)
